TPU v7x, 256 devices: a whole 4x4x8 slice. The times are simulated.
256 devices in a mesh: fsdp: 32 (over z, y), tp: 8 (over x, core).
Axes of the slice: x: 4, y: 4, z: 8, core: 2. Of those that a mesh axis runs over, the one named last changes fastest.
Arguments:
- tokens: bfloat16 [8192, 4096], P('fsdp', 'tp'), may hold values from -6 to 6
- cotangent: bfloat16 [8192, 4096], P('fsdp', 'tp'), may hold values from -6 to 6
- up_weight: bfloat16 [4096, 14336], P('fsdp', 'tp'), may hold values from -0.1875 to 0.1875
- down_weight: bfloat16 [4096, 14336], P('fsdp', 'tp'), may hold values from -0.09375 to 0.09375
- up_list: int32 [8, 128, 2], P('tp'), may hold values from 0 to 31, as said below
- up_count: int32 [8], P('tp'), may hold values from 35 to 128, as said below
- down_list: int32 [8, 128, 2], P('tp'), may hold values from 0 to 31, as said below
- down_count: int32 [8], P('tp'), may hold values from 35 to 128, as said below
Outputs:
- mixed: bfloat16 [8192, 4096], P('fsdp', 'tp')
- grad_tokens: bfloat16 [8192, 4096], P('fsdp', 'tp')
- grad_up: float32 [4096, 14336], P('fsdp', 'tp')
- grad_down: float32 [4096, 14336], P('fsdp', 'tp')
Inputs may be any that keep to these rules, and one draw needn't show every extreme that they name: `up_list`: in each slice's list the first count entries are distinct pairs (row block below 32, column block below 14), in no particular order; every row block has at least one and at most 4 of them; in every slice the one row block held by some index of fsdp have exactly 4, and in some slice every row block has exactly 4. Entries from the count on are arbitrary pairs in range and carry no meaning. `up_count`: the number of valid entries of each slice's up list. `down_list`: as for up_list. `down_count`: the number of valid entries of each slice's down list.
All inputs are finite; a program needn't handle non-finite values.
Results may differ from a plain program's by a relative error of at most 0.015.
Values may be sent and summed in bfloat16 or wider, within the bound.
No kernel may reach another device: no remote copies, remote signals or barrier semaphores. Data moves between devices by JAX's collectives and lax.ppermute only.
A program may use at most 256 MiB of HBM per device.

v0:
```python
import jax
import jax.numpy as jnp
from jax import lax
from jax.sharding import PartitionSpec as P

BLK = 128
SQRT_TWO_PI = 0.7978845608028654
CUBIC = 0.044715


def gelu_tanh(values):
    inner = SQRT_TWO_PI * (values + CUBIC * values * values * values)
    return 0.5 * values * (1.0 + jnp.tanh(inner))


def gelu_slope(values):
    tangent = jnp.tanh(SQRT_TWO_PI * (values + CUBIC * values * values * values))
    return 0.5 * (1.0 + tangent) + 0.5 * values * (1.0 - tangent * tangent) * SQRT_TWO_PI * (
        1.0 + 3.0 * CUBIC * values * values
    )


def list_table(entries, number):
    valid = jnp.arange(entries.shape[0], dtype=jnp.int32) < number
    return (entries[:, 0], entries[:, 1], valid)


def slot_table(entries, number, owner_blocks, owners, capacity):
    rows, cols, valid = list_table(entries, number)
    owner = rows // owner_blocks
    member = (
        (owner[:, None] == jnp.arange(owners, dtype=jnp.int32)[None, :]) & valid[:, None]
    ).astype(jnp.int32)
    earlier = jnp.cumsum(member, axis=0) - member
    rank = jnp.sum(earlier * member, axis=1)
    slot = owner * capacity + rank
    chosen = (
        valid[:, None] & (slot[:, None] == jnp.arange(owners * capacity, dtype=jnp.int32)[None, :])
    ).astype(jnp.int32)
    slot_rows = jnp.sum(chosen * rows[:, None], axis=0)
    slot_cols = jnp.sum(chosen * cols[:, None], axis=0)
    slot_valid = jnp.sum(chosen, axis=0) > 0
    return (slot_rows, slot_cols, slot_valid)


def pick_blocks(weight, table, row_offset):
    rows, cols, valid = table
    row_count = weight.shape[0] // BLK
    col_count = weight.shape[1] // BLK
    tiles = weight.reshape(row_count, BLK, col_count, BLK)
    local_rows = jnp.clip(rows - row_offset, 0, row_count - 1)
    picked = tiles[local_rows, :, cols, :]
    return jnp.where(valid[:, None, None], picked, jnp.zeros((), weight.dtype))


def place_grads(tiles, table, first_block, block_count, col_blocks):
    rows, cols, valid = table
    inside = valid & (rows >= first_block) & (rows < first_block + block_count)
    local_rows = jnp.clip(rows - first_block, 0, block_count - 1)
    kept = jnp.where(inside[:, None, None], tiles, jnp.zeros((), jnp.float32))
    spread = (
        jnp.zeros((block_count, BLK, col_blocks, BLK), jnp.float32)
        .at[local_rows, :, cols, :]
        .add(kept)
    )
    return spread.reshape(block_count * BLK, col_blocks * BLK)


def fetch(up_weight, down_weight, up_table, down_table, capacity, owner_blocks):
    first_slot = lax.axis_index("fsdp") * capacity
    up_mine = tuple((lax.dynamic_slice_in_dim(member, first_slot, capacity) for member in up_table))
    down_mine = tuple(
        (lax.dynamic_slice_in_dim(member, first_slot, capacity) for member in down_table)
    )
    offset = lax.axis_index("fsdp") * owner_blocks
    return (
        lax.all_gather(pick_blocks(up_weight, up_mine, offset), "fsdp", axis=0, tiled=True),
        lax.all_gather(pick_blocks(down_weight, down_mine, offset), "fsdp", axis=0, tiled=True),
    )


def body(tokens, cotangent, up_weight, down_weight, up_list, up_count, down_list, down_count):
    owner_blocks = up_weight.shape[0] // BLK
    col_blocks = up_weight.shape[1] // BLK
    owners = lax.axis_size("fsdp")
    group_rows = tokens.shape[0]
    up_table = slot_table(
        up_list[0],
        up_count[0],
        owner_blocks,
        owners,
        owner_blocks * (up_list.shape[1] // (owners * owner_blocks)),
    )
    down_table = slot_table(
        down_list[0],
        down_count[0],
        owner_blocks,
        owners,
        owner_blocks * (down_list.shape[1] // (owners * owner_blocks)),
    )
    capacity = up_list.shape[1] // owners
    up_blocks, down_blocks = fetch(
        up_weight, down_weight, up_table, down_table, capacity, owner_blocks
    )
    gathered = lax.all_gather(tokens, "tp", axis=1, tiled=True)
    width = gathered.shape[1]
    row_blocks = width // BLK
    x_tiles = gathered.reshape(group_rows, row_blocks, BLK)
    x_taken = jnp.take(x_tiles, up_table[0], axis=1)
    partial_up = jnp.einsum("rsk,skn->rsn", x_taken, up_blocks, preferred_element_type=jnp.float32)
    hidden = (
        jnp.zeros((group_rows, col_blocks, BLK), jnp.float32).at[:, up_table[1], :].add(partial_up)
    )
    active = gelu_tanh(hidden).astype(jnp.bfloat16)
    active_taken = jnp.take(active, down_table[1], axis=1)
    layer_product = jnp.einsum(
        "rsn,skn->rsk", active_taken, down_blocks, preferred_element_type=jnp.float32
    )
    layer_parts = (
        jnp.zeros((group_rows, row_blocks, BLK), jnp.float32)
        .at[:, down_table[0], :]
        .add(layer_product)
    )
    mixed = lax.psum_scatter(
        layer_parts.reshape(group_rows, width).astype(jnp.bfloat16),
        "tp",
        scatter_dimension=1,
        tiled=True,
    )
    up_again, down_again = fetch(
        up_weight, down_weight, up_table, down_table, capacity, owner_blocks
    )
    grad_in = lax.all_gather(cotangent, "tp", axis=1, tiled=True)
    dy_tiles = grad_in.reshape(group_rows, row_blocks, BLK)
    dy_taken = jnp.take(dy_tiles, down_table[0], axis=1)
    back_down = jnp.einsum("rsk,skn->rsn", dy_taken, down_again, preferred_element_type=jnp.float32)
    grad_active = (
        jnp.zeros((group_rows, col_blocks, BLK), jnp.float32).at[:, down_table[1], :].add(back_down)
    )
    grad_hidden = (grad_active * gelu_slope(hidden)).astype(jnp.bfloat16)
    hidden_taken = jnp.take(grad_hidden, up_table[1], axis=1)
    back_up = jnp.einsum("rsn,skn->rsk", hidden_taken, up_again, preferred_element_type=jnp.float32)
    input_parts = (
        jnp.zeros((group_rows, row_blocks, BLK), jnp.float32).at[:, up_table[0], :].add(back_up)
    )
    grad_tokens = lax.psum_scatter(
        input_parts.reshape(group_rows, width).astype(jnp.bfloat16),
        "tp",
        scatter_dimension=1,
        tiled=True,
    )
    up_rows_part = up_table[0]
    up_cols_part = up_table[1]
    down_rows_part = down_table[0]
    down_cols_part = down_table[1]
    x_part = jnp.take(x_tiles, up_rows_part, axis=1)
    hidden_part = jnp.take(grad_hidden, up_cols_part, axis=1)
    dy_part = jnp.take(dy_tiles, down_rows_part, axis=1)
    active_part = jnp.take(active, down_cols_part, axis=1)
    up_term = jnp.einsum("rsk,rsn->skn", x_part, hidden_part, preferred_element_type=jnp.float32)
    down_term = jnp.einsum("rsk,rsn->skn", dy_part, active_part, preferred_element_type=jnp.float32)
    summed = lax.psum_scatter(
        jnp.stack([up_term, down_term], axis=1).astype(jnp.bfloat16),
        "fsdp",
        scatter_dimension=0,
        tiled=True,
    ).astype(jnp.float32)
    first_slot = lax.axis_index("fsdp") * capacity
    offset = lax.axis_index("fsdp") * owner_blocks
    up_mine = tuple((lax.dynamic_slice_in_dim(member, first_slot, capacity) for member in up_table))
    down_mine = tuple(
        (lax.dynamic_slice_in_dim(member, first_slot, capacity) for member in down_table)
    )
    grad_up = place_grads(summed[:, 0], up_mine, offset, owner_blocks, col_blocks)
    grad_down = place_grads(summed[:, 1], down_mine, offset, owner_blocks, col_blocks)
    return (mixed, grad_tokens, grad_up, grad_down)


def solution(mesh):
    return jax.shard_map(
        body,
        mesh=mesh,
        in_specs=(
            P("fsdp", "tp"),
            P("fsdp", "tp"),
            P("fsdp", "tp"),
            P("fsdp", "tp"),
            P("tp", None, None),
            P("tp"),
            P("tp", None, None),
            P("tp"),
        ),
        out_specs=(P("fsdp", "tp"), P("fsdp", "tp"), P("fsdp", "tp"), P("fsdp", "tp")),
        check_vma=False,
    )
```

profile of v0, /device:TPU:1, one launch (start us, length us, event | category | flops | bytes accessed | tf_op | source)
XLA Modules:
  0.0 681.6 jit_solution(12440131534698281654)
XLA Ops:
  24.6 17.8 %all-gather.9.cloned.1.call-done = bf16[256,4096]{0,1:T(8,128)(2,1)} async-done(((bf16[256,512]{0,1:T(8,128)(2,1)}), bf16[256,4096]{0,1:T(8,128)(2,1)}) %all-gather.9.cloned.1.call-update) | async-done | bytes 2097168 | tf_op jit(solution)/shard_map/all_gather | solution.py:105
  42.5 3.2 copy.65
  45.7 27.4 %all-gather.11.cloned.1.call-done = bf16[256,4096]{0,1:T(8,128)(2,1)} async-done(((bf16[256,512]{0,1:T(8,128)(2,1)}), bf16[256,4096]{0,1:T(8,128)(2,1)}) %all-gather.11.cloned.1.call-update) | async-done | bytes 2097168 | tf_op jit(solution)/shard_map/all_gather | solution.py:133
  73.1 4.1 copy.72
  77.2 6.5 gather_fusion.2
  83.7 8.1 %gather_fusion.4 = bf16[128,256,128]{2,1,0:T(8,128)(2,1)} fusion(bf16[256,32,128]{2,0,1:T(8,128)(2,1)} %copy.72, s32[1024]{0:T(1024)S(1)} %pad_clamp_fusion.1), kind=kCustom, calls=%fused_computation.2.clone | custom fusion | bytes 16777728 | tf_op jit(solution)/shard_map/jit(_take)/gather | solution.py:135
  91.8 62.8 %all-gather.7.cloned.1.call-done = bf16[128,128,128]{2,1,0:T(8,128)(2,1)} async-done(((bf16[4,128,128]{2,1,0:T(8,128)(2,1)}), bf16[128,128,128]{2,1,0:T(8,128)(2,1)}) %all-gather.7.cloned.1.call-update) | async-done | bytes 4194320 | tf_op jit(solution)/shard_map/all_gather | solution.py:77
  154.6 12.7 %fusion.12 = f32[128,256,128]{2,1,0:T(8,128)} fusion(bf16[128,128,128]{2,1,0:T(8,128)(2,1)} %all-gather.7.cloned.1.call-done, bf16[128,256,128]{2,1,0:T(8,128)(2,1)} %gather_fusion.2, pred[128]{0:T(512)(128)(4,1)S(1)} %get-tuple-element.49), kind=kOutput, calls=%fused_computation.25 | convolution fusion | flops 1077936128 | bytes 29360256 | tf_op jit(solution)/shard_map/rsk,skn->rsn/dot_general | solution.py:110
  167.4 24.3 %scatter_fusion = f32[256,14,128]{2,0,1:T(8,128)S(1)} fusion(f32[256,14,128]{2,0,1:T(8,128)S(1)} %broadcast.166.clone.1, s32[128]{0:T(128)S(1)} %fusion.38, f32[128,256,128]{2,1,0:T(8,128)} %fusion.12), kind=kCustom, calls=%fused_computation.6 | custom fusion | flops 4194304 | bytes 50332160 | tf_op jit(solution)/shard_map/scatter-add | solution.py:112
  191.7 44.5 %all-gather.5.cloned.1.call-done = bf16[128,128,128]{2,1,0:T(8,128)(2,1)} async-done(((bf16[4,128,128]{2,1,0:T(8,128)(2,1)}), bf16[128,128,128]{2,1,0:T(8,128)(2,1)}) %all-gather.5.cloned.1.call-update) | async-done | bytes 4194320 | tf_op jit(solution)/shard_map/all_gather | solution.py:78
  236.2 12.7 %fusion.6 = f32[128,256,128]{2,1,0:T(8,128)} fusion(bf16[128,128,128]{2,1,0:T(8,128)(2,1)} %all-gather.5.cloned.1.call-done, bf16[128,256,128]{2,1,0:T(8,128)(2,1)} %gather_fusion.4, pred[128]{0:T(512)(128)(4,1)S(1)} %get-tuple-element.44), kind=kOutput, calls=%fused_computation.19 | convolution fusion | flops 1077936128 | bytes 29360256 | tf_op jit(solution)/shard_map/rsk,skn->rsn/dot_general | solution.py:136
  250.4 36.6 %scatter_fusion.2 = f32[256,14,128]{2,0,1:T(8,128)} fusion(f32[256,14,128]{2,0,1:T(8,128)} %broadcast.166.clone, s32[128]{0:T(128)S(1)} %fusion.40, f32[128,256,128]{2,1,0:T(8,128)} %fusion.6), kind=kCustom, calls=%fused_computation.8 | custom fusion | flops 4194304 | bytes 50332160 | tf_op jit(solution)/shard_map/scatter-add | solution.py:138
  287.0 3.7 fusion.28
  290.7 7.7 %gather_fusion.5 = bf16[128,256,128]{2,1,0:T(8,128)(2,1)} fusion(bf16[256,14,128]{2,0,1:T(8,128)(2,1)} %get-tuple-element.36, s32[1024]{0:T(1024)S(1)} %pad_clamp_fusion), kind=kCustom, calls=%fused_computation.3.clone | custom fusion | bytes 16777728 | tf_op jit(solution)/shard_map/jit(_take)/gather | solution.py:141
  298.4 12.7 %fusion.2 = f32[128,256,128]{2,1,0:T(8,128)} fusion(bf16[128,128,128]{2,1,0:T(8,128)(2,1)} %all-gather.7.cloned.1.call-done, bf16[128,256,128]{2,1,0:T(8,128)(2,1)} %gather_fusion.5, pred[128]{0:T(512)(128)(4,1)S(1)} %get-tuple-element.48), kind=kOutput, calls=%fused_computation.15 | convolution fusion | flops 1077936128 | bytes 29360256 | tf_op jit(solution)/shard_map/rsn,skn->rsk/dot_general | solution.py:142
  311.1 2.4 broadcast.160.clone.1
  313.5 35.7 %scatter_fusion.3 = f32[256,32,128]{2,0,1:T(8,128)} fusion(f32[256,32,128]{2,0,1:T(8,128)} %broadcast.160.clone.1, s32[128]{0:T(128)S(1)} %fusion.39, f32[128,256,128]{2,1,0:T(8,128)} %fusion.2), kind=kCustom, calls=%fused_computation.9 | custom fusion | flops 4194304 | bytes 50332160 | tf_op jit(solution)/shard_map/scatter-add | solution.py:144
  349.1 2.5 convert_element_type.42
  351.6 2.9 copy.73
  354.6 6.7 gather_fusion.3
  361.4 12.7 %fusion.9 = f32[128,256,128]{2,1,0:T(8,128)} fusion(bf16[128,128,128]{2,1,0:T(8,128)(2,1)} %all-gather.5.cloned.1.call-done, bf16[128,256,128]{2,1,0:T(8,128)(2,1)} %gather_fusion.3, pred[128]{0:T(512)(128)(4,1)S(1)} %get-tuple-element.45), kind=kOutput, calls=%fused_computation.22 | convolution fusion | flops 1077936128 | bytes 29360256 | tf_op jit(solution)/shard_map/rsn,skn->rsk/dot_general | solution.py:116
  374.1 2.5 broadcast.160.clone
  376.6 35.8 %scatter_fusion.1 = f32[256,32,128]{2,0,1:T(8,128)} fusion(f32[256,32,128]{2,0,1:T(8,128)} %broadcast.160.clone, s32[128]{0:T(128)S(1)} %fusion.37, f32[128,256,128]{2,1,0:T(8,128)} %fusion.9), kind=kCustom, calls=%fused_computation.7 | custom fusion | flops 4194304 | bytes 50332160 | tf_op jit(solution)/shard_map/scatter-add | solution.py:122
  412.4 2.5 convert_element_type.39
  414.9 2.9 copy.70
  417.9 8.1 %convert_bitcast_fusion = bf16[128,1,128,128]{3,2,0,1:T(8,128)(2,1)S(1)} fusion(bf16[128,256,128]{2,1,0:T(8,128)(2,1)} %gather_fusion.3, pred[128]{0:T(512)(128)(4,1)S(1)} %get-tuple-element.45, bf16[128,256,128]{2,1,0:T(8,128)(2,1)} %gather_fusion.4, pred[128]{0:T(512)(128)(4,1)S(1)} %get-tuple-element.44), kind=kOutput, calls=%fused_computation.31 | convolution fusion | flops 1084227584 | bytes 20971776 | tf_op jit(solution)/shard_map/rsk,rsn->skn/dot_general | solution.py:161
  426.0 9.3 %convert_bitcast_fusion.1 = bf16[128,1,128,128]{3,2,0,1:T(8,128)(2,1)} fusion(bf16[128,256,128]{2,1,0:T(8,128)(2,1)} %gather_fusion.5, pred[128]{0:T(512)(128)(4,1)S(1)} %get-tuple-element.48, bf16[128,256,128]{2,1,0:T(8,128)(2,1)} %gather_fusion.2, pred[128]{0:T(512)(128)(4,1)S(1)} %get-tuple-element.49), kind=kOutput, calls=%fused_computation.32 | convolution fusion | flops 1084227584 | bytes 20971776 | tf_op jit(solution)/shard_map/rsk,rsn->skn/dot_general | solution.py:160
  435.2 6.3 pad_maximum_fusion
  443.4 1.8 copy.79
  445.2 7.0 %reduce-scatter.6.cloned.1.call-done = bf16[256,512]{0,1:T(8,128)(2,1)} async-done(((bf16[256,4096]{0,1:T(8,128)(2,1)}), bf16[256,512]{0,1:T(8,128)(2,1)}) %reduce-scatter.6.cloned.1.call-update) | async-done | bytes 262160 | tf_op jit(solution)/shard_map/reduce_scatter | solution.py:124
  452.2 1.8 copy.78
  454.0 214.8 %all-reduce.3.cloned.1.call-done = bf16[128,2,128,128]{3,2,0,1:T(8,128)(2,1)} async-done(((bf16[128,2,128,128]{3,2,0,1:T(8,128)(2,1)}), bf16[128,2,128,128]{3,2,0,1:T(8,128)(2,1)}) %all-reduce.3.cloned.1.call-update) | async-done | bytes 8388624
  (83 shorter events, 24.7 us)
Async XLA Ops:
  7.2 35.3 %all-gather.9.cloned.1.call-start = ((), (), s32[]{:S(2)}) async-start(), calls=%async_computation.4 | async-start | bytes 2359296 | tf_op jit(solution)/shard_map/all_gather | solution.py:105
  9.0 64.1 %all-gather.11.cloned.1.call-start = ((), (), s32[]{:S(2)}) async-start(), calls=%async_computation.6 | async-start | bytes 2359296 | tf_op jit(solution)/shard_map/all_gather | solution.py:133
  10.9 143.7 %all-gather.7.cloned.1.call-start = ((), (), s32[]{:S(2)}) async-start(), calls=%async_computation.3 | async-start | bytes 4325376 | tf_op jit(solution)/shard_map/all_gather | solution.py:77
  20.6 215.6 %all-gather.5.cloned.1.call-start = ((), (), s32[]{:S(2)}) async-start(), calls=%async_computation.2 | async-start | bytes 4325376 | tf_op jit(solution)/shard_map/all_gather | solution.py:78
  24.3 419.2 %reduce-scatter.8.cloned.1.call-start = ((), (), s32[]{:S(2)}) async-start(), calls=%async_computation.7 | async-start | bytes 2359296 | tf_op jit(solution)/shard_map/reduce_scatter | solution.py:146
  354.6 97.7 %reduce-scatter.6.cloned.1.call-start = ((), (), s32[]{:S(2)}) async-start(), calls=%async_computation.5 | async-start | bytes 2359296 | tf_op jit(solution)/shard_map/reduce_scatter | solution.py:124
  417.8 251.0 %all-reduce.3.cloned.1.call-start = ((), (), s32[]{:S(2)}) async-start(), calls=%async_computation.8 | async-start | bytes 16777216
  441.5 0.7 copy-start.4
  441.5 228.3 %copy-start = (pred[4]{0:T(512)(128)(4,1)S(1)}, pred[4]{0:T(512)(128)(4,1)}, u32[]{:S(2)}) copy-start(pred[4]{0:T(512)(128)(4,1)} %get-tuple-element.32) | copy-start | bytes 16
  441.5 228.3 %copy-start.1 = (pred[4]{0:T(512)(128)(4,1)S(1)}, pred[4]{0:T(512)(128)(4,1)}, u32[]{:S(2)}) copy-start(pred[4]{0:T(512)(128)(4,1)} %get-tuple-element.28) | copy-start | bytes 16
  441.5 228.5 %copy-start.3 = (s32[4]{0:T(128)S(1)}, s32[4]{0:T(128)}, u32[]{:S(2)}) copy-start(s32[4]{0:T(128)} %get-tuple-element.30) | copy-start | bytes 52
  441.5 230.9 %copy-start.2 = (s32[4]{0:T(128)S(1)}, s32[4]{0:T(128)}, u32[]{:S(2)}) copy-start(s32[4]{0:T(128)} %get-tuple-element.46) | copy-start | bytes 52
Sparse Core Ops, SparseCore 0:
  10.4 32.0 all-gather.8
  44.9 28.1 all-gather.10
  76.2 78.3 all-gather.6
  157.6 78.5 all-gather.4
  354.7 34.2 reduce-scatter.7
  417.9 34.2 reduce-scatter.5
  455.9 212.8 all-reduce.2
where the time goes:
time: 683 us; the launch traced here: 682 us
  waiting for transfers between devices  375 us (55%)
  other arithmetic  156 us (23%)
  matrix products  68.1 us (10%)
  local copies, waits for them, and re-layouts  66 us (10%)
  between operations  16.4 us (2%)
    unnamed x8, waiting for transfers between devices  215 us
    all_gather x1, waiting for transfers between devices, fetch(): lax.all_gather(pick_blocks(up_weight, up_mine, offset), 'fsdp', axis=0, t...  62.8 us
    all_gather x1, waiting for transfers between devices, fetch(): lax.all_gather(pick_blocks(down_weight, down_mine, offset), 'fsdp', axis=...  44.5 us
    scatter-add x1, other arithmetic, body(): jnp.zeros((group_rows, col_blocks, BLK), jnp.float32)  36.6 us
    scatter-add x1, other arithmetic, body(): layer_parts = jnp.zeros((group_rows, row_blocks, BLK), jnp.float32).at[:,...  35.8 us
    scatter-add x1, other arithmetic, body(): jnp.zeros((group_rows, row_blocks, BLK), jnp.float32).at[:, up_table[0], :]  35.7 us
    all_gather x1, waiting for transfers between devices, body(): grad_in = lax.all_gather(cotangent, 'tp', axis=1, tiled=True)  27.4 us
    scatter-add x1, other arithmetic, body(): jnp.zeros((group_rows, col_blocks, BLK), jnp.float32).at[:, up_table[1], :]  24.3 us
  transfers between devices with their start and end apart: 7, of which 6 were waited for; matrix products, arithmetic and copies ran while one was open for 24% of the time, Pallas kernels for 0%

commit v1 on v0

--- a/solution.py
+++ b/solution.py
@@ -6,6 +6,11 @@
 BLK = 128
 SQRT_TWO_PI = 0.7978845608028654
 CUBIC = 0.044715
+
+
+def gather_over(x, axis, dim):
+    sent = jnp.stack([x] * lax.axis_size(axis))
+    return jnp.concatenate(lax.all_to_all(sent, axis, 0, 0), axis=dim)
 
 
 def gelu_tanh(values):
@@ -75,7 +80,7 @@
     offset = lax.axis_index("fsdp") * owner_blocks
     return (
         lax.all_gather(pick_blocks(up_weight, up_mine, offset), "fsdp", axis=0, tiled=True),
-        lax.all_gather(pick_blocks(down_weight, down_mine, offset), "fsdp", axis=0, tiled=True),
+        gather_over(pick_blocks(down_weight, down_mine, offset), "fsdp", 0),
     )
 
 

time: 683 us -> 617 us (0.903)
  waiting for transfers between devices: 375 us -> 295 us
  starting transfers between devices: 0.47 us -> 12.6 us
    all_gather x1, waiting for transfers between devices: 62.8 us -> 0.02 us  [fetch(): lax.all_gather(pick_blocks(up_weight, up_mine, offset), 'fsdp', axis=0, t...]
    all_gather x1 -> x0, waiting for transfers between devices: 44.5 us -> none  [fetch(): lax.all_gather(pick_blocks(down_weight, down_mine, offset), 'fsdp', axis=...]
    all_to_all x0 -> x1, waiting for transfers between devices: none -> 40.8 us  [gather_over(): return jnp.concatenate(lax.all_to_all(sent, axis, 0, 0), axis=dim)]
    all_gather x1, waiting for transfers between devices: 27.4 us -> 4.36 us  [body(): grad_in = lax.all_gather(cotangent, 'tp', axis=1, tiled=True)]
    scatter-add x1, other arithmetic: 24.3 us -> 36.7 us  [body(): jnp.zeros((group_rows, col_blocks, BLK), jnp.float32).at[:, up_table[1], :]]
    scatter-add x1, other arithmetic: 36.6 us -> 24.4 us  [body(): jnp.zeros((group_rows, col_blocks, BLK), jnp.float32)]
    all_to_all x0 -> x1, starting transfers between devices: none -> 12.2 us  [gather_over(): return jnp.concatenate(lax.all_to_all(sent, axis, 0, 0), axis=dim)]
    all_gather x1, waiting for transfers between devices: 17.8 us -> 27.5 us  [body(): gathered = lax.all_gather(tokens, 'tp', axis=1, tiled=True)]
  transfers between devices with their start and end apart: 7 -> 7, of which waited for: 6 -> 5; matrix products, arithmetic and copies ran while one was open for 24% -> 27% of each run, Pallas kernels for 0% -> 0%
where the time goes in v1:
time: 617 us; the launch traced here: 616 us
  waiting for transfers between devices  295 us (48%)
  other arithmetic  156 us (25%)
  matrix products  68.5 us (11%)
  local copies, waits for them, and re-layouts  68 us (11%)
  between operations  16.4 us (3%)
  starting transfers between devices  12.6 us (2%)
    unnamed x7, waiting for transfers between devices  215 us
    all_to_all x1, waiting for transfers between devices, gather_over(): return jnp.concatenate(lax.all_to_all(sent, axis, 0, 0), axis=dim)  40.8 us
    scatter-add x1, other arithmetic, body(): jnp.zeros((group_rows, col_blocks, BLK), jnp.float32).at[:, up_table[1], :]  36.7 us
    scatter-add x1, other arithmetic, body(): layer_parts = jnp.zeros((group_rows, row_blocks, BLK), jnp.float32).at[:,...  35.8 us
    scatter-add x1, other arithmetic, body(): jnp.zeros((group_rows, row_blocks, BLK), jnp.float32).at[:, up_table[0], :]  35.7 us
    all_gather x1, waiting for transfers between devices, body(): gathered = lax.all_gather(tokens, 'tp', axis=1, tiled=True)  27.5 us
    scatter-add x1, other arithmetic, body(): jnp.zeros((group_rows, col_blocks, BLK), jnp.float32)  24.4 us
    dot_general x1, matrix products, body(): jnp.einsum('rsk,skn->rsn', dy_taken, down_again, preferred_element_type=j...  13.1 us
  transfers between devices with their start and end apart: 7, of which 5 were waited for; matrix products, arithmetic and copies ran while one was open for 27% of the time, Pallas kernels for 0%

profile of v1, /device:TPU:1, one launch (start us, length us, event | category | flops | bytes accessed | tf_op | source)
XLA Modules:
  0.0 615.8 jit_solution(399774376689263751)
XLA Ops:
  9.1 1.8 copy.64
  19.9 3.0 stack.11
  22.9 12.2 %all-to-all-start = ((bf16[32,4,128,128]{3,2,1,0:T(8,128)(2,1)}), bf16[32,4,128,128]{3,2,1,0:T(8,128)(2,1)}, u32[]{:S(2)}, u32[]{:S(2)}) async-start(bf16[32,4,128,128]{3,2,1,0:T(8,128)(2,1)} %stack.11), calls=%async_computation | async-start | bytes 8388608 | tf_op jit(solution)/shard_map/all_to_all | solution.py:13
  38.1 4.4 all-gather.8.cloned.1.call-done
  42.5 3.2 copy.72
  45.7 27.5 %all-gather.6.cloned.1.call-done = bf16[256,4096]{0,1:T(8,128)(2,1)} async-done(((bf16[256,512]{0,1:T(8,128)(2,1)}), bf16[256,4096]{0,1:T(8,128)(2,1)}) %all-gather.6.cloned.1.call-update) | async-done | bytes 2097168 | tf_op jit(solution)/shard_map/all_gather | solution.py:110
  73.2 4.1 copy.65
  77.2 6.5 %gather_fusion.4 = bf16[128,256,128]{2,1,0:T(8,128)(2,1)} fusion(bf16[256,32,128]{2,0,1:T(8,128)(2,1)S(1)} %copy.72, s32[1024]{0:T(1024)S(1)} %pad_clamp_fusion.1), kind=kCustom, calls=%fused_computation.2.clone | custom fusion | bytes 16777728 | tf_op jit(solution)/shard_map/jit(_take)/gather | solution.py:140
  83.7 8.1 %gather_fusion.2 = bf16[128,256,128]{2,1,0:T(8,128)(2,1)} fusion(bf16[256,32,128]{2,0,1:T(8,128)(2,1)} %copy.65, s32[1024]{0:T(1024)S(1)} %pad_clamp_fusion.3), kind=kCustom, calls=%fused_computation.clone | custom fusion | bytes 16777728 | tf_op jit(solution)/shard_map/jit(_take)/gather | solution.py:114
  91.8 40.8 %all-to-all-done = bf16[32,4,128,128]{3,2,1,0:T(8,128)(2,1)} async-done(((bf16[32,4,128,128]{3,2,1,0:T(8,128)(2,1)}), bf16[32,4,128,128]{3,2,1,0:T(8,128)(2,1)}, u32[]{:S(2)}, u32[]{:S(2)}) %all-to-all-start) | async-done | bytes 4194336 | tf_op jit(solution)/shard_map/all_to_all | solution.py:13
  132.7 13.1 %fusion.6 = f32[128,256,128]{2,1,0:T(8,128)} fusion(bf16[128,128,128]{2,1,0:T(8,128)(2,1)} %bitcast.21, bf16[128,256,128]{2,1,0:T(8,128)(2,1)} %gather_fusion.4, pred[128]{0:T(512)(128)(4,1)S(1)} %get-tuple-element.44), kind=kOutput, calls=%fused_computation.19 | convolution fusion | flops 1077936128 | bytes 29360256 | tf_op jit(solution)/shard_map/rsk,skn->rsn/dot_general | solution.py:141
  145.9 24.4 %scatter_fusion.2 = f32[256,14,128]{2,0,1:T(8,128)S(1)} fusion(f32[256,14,128]{2,0,1:T(8,128)S(1)} %broadcast.171.clone, s32[128]{0:T(128)S(1)} %fusion.40, f32[128,256,128]{2,1,0:T(8,128)} %fusion.6), kind=kCustom, calls=%fused_computation.8 | custom fusion | flops 4194304 | bytes 50332160 | tf_op jit(solution)/shard_map/scatter-add | solution.py:143
  170.4 12.7 %fusion.12 = f32[128,256,128]{2,1,0:T(8,128)} fusion(bf16[128,128,128]{2,1,0:T(8,128)(2,1)} %all-gather.4.cloned.1.call-done, bf16[128,256,128]{2,1,0:T(8,128)(2,1)} %gather_fusion.2, pred[128]{0:T(512)(128)(4,1)S(1)} %get-tuple-element.49), kind=kOutput, calls=%fused_computation.25 | convolution fusion | flops 1077936128 | bytes 29360256 | tf_op jit(solution)/shard_map/rsk,skn->rsn/dot_general | solution.py:115
  184.5 36.7 %scatter_fusion = f32[256,14,128]{2,0,1:T(8,128)} fusion(f32[256,14,128]{2,0,1:T(8,128)} %broadcast.171.clone.1, s32[128]{0:T(128)S(1)} %fusion.38, f32[128,256,128]{2,1,0:T(8,128)} %fusion.12), kind=kCustom, calls=%fused_computation.6 | custom fusion | flops 4194304 | bytes 50332160 | tf_op jit(solution)/shard_map/scatter-add | solution.py:117
  221.2 3.7 fusion.28
  225.0 7.7 %gather_fusion.5 = bf16[128,256,128]{2,1,0:T(8,128)(2,1)} fusion(bf16[256,14,128]{2,0,1:T(8,128)(2,1)} %get-tuple-element.36, s32[1024]{0:T(1024)S(1)} %pad_clamp_fusion), kind=kCustom, calls=%fused_computation.3.clone | custom fusion | bytes 16777728 | tf_op jit(solution)/shard_map/jit(_take)/gather | solution.py:146
  232.6 12.7 %fusion.2 = f32[128,256,128]{2,1,0:T(8,128)} fusion(bf16[128,128,128]{2,1,0:T(8,128)(2,1)} %all-gather.4.cloned.1.call-done, bf16[128,256,128]{2,1,0:T(8,128)(2,1)} %gather_fusion.5, pred[128]{0:T(512)(128)(4,1)S(1)} %get-tuple-element.48), kind=kOutput, calls=%fused_computation.15 | convolution fusion | flops 1077936128 | bytes 29360256 | tf_op jit(solution)/shard_map/rsn,skn->rsk/dot_general | solution.py:147
  245.3 2.4 broadcast.165.clone.1
  247.7 35.7 %scatter_fusion.3 = f32[256,32,128]{2,0,1:T(8,128)} fusion(f32[256,32,128]{2,0,1:T(8,128)} %broadcast.165.clone.1, s32[128]{0:T(128)S(1)} %fusion.39, f32[128,256,128]{2,1,0:T(8,128)} %fusion.2), kind=kCustom, calls=%fused_computation.9 | custom fusion | flops 4194304 | bytes 50332160 | tf_op jit(solution)/shard_map/scatter-add | solution.py:149
  283.4 2.5 convert_element_type.42
  285.9 2.9 copy.73
  288.9 6.7 %gather_fusion.3 = bf16[128,256,128]{2,1,0:T(8,128)(2,1)} fusion(bf16[256,14,128]{2,0,1:T(8,128)(2,1)S(1)} %get-tuple-element.37, s32[1024]{0:T(1024)S(1)} %pad_clamp_fusion.2), kind=kCustom, calls=%fused_computation.1.clone | custom fusion | bytes 16777728 | tf_op jit(solution)/shard_map/jit(_take)/gather | solution.py:120
  295.6 12.7 %fusion.9 = f32[128,256,128]{2,1,0:T(8,128)} fusion(bf16[128,128,128]{2,1,0:T(8,128)(2,1)} %bitcast.21, bf16[128,256,128]{2,1,0:T(8,128)(2,1)} %gather_fusion.3, pred[128]{0:T(512)(128)(4,1)S(1)} %get-tuple-element.45), kind=kOutput, calls=%fused_computation.22 | convolution fusion | flops 1077936128 | bytes 29360256 | tf_op jit(solution)/shard_map/rsn,skn->rsk/dot_general | solution.py:121
  308.3 2.5 broadcast.165.clone
  310.9 35.8 %scatter_fusion.1 = f32[256,32,128]{2,0,1:T(8,128)} fusion(f32[256,32,128]{2,0,1:T(8,128)} %broadcast.165.clone, s32[128]{0:T(128)S(1)} %fusion.37, f32[128,256,128]{2,1,0:T(8,128)} %fusion.9), kind=kCustom, calls=%fused_computation.7 | custom fusion | flops 4194304 | bytes 50332160 | tf_op jit(solution)/shard_map/scatter-add | solution.py:127
  346.6 2.5 convert_element_type.39
  349.1 2.9 copy.70
  352.1 8.1 %convert_bitcast_fusion = bf16[128,1,128,128]{3,2,0,1:T(8,128)(2,1)S(1)} fusion(bf16[128,256,128]{2,1,0:T(8,128)(2,1)} %gather_fusion.3, pred[128]{0:T(512)(128)(4,1)S(1)} %get-tuple-element.45, bf16[128,256,128]{2,1,0:T(8,128)(2,1)} %gather_fusion.4, pred[128]{0:T(512)(128)(4,1)S(1)} %get-tuple-element.44), kind=kOutput, calls=%fused_computation.31 | convolution fusion | flops 1084227584 | bytes 20971776 | tf_op jit(solution)/shard_map/rsk,rsn->skn/dot_general | solution.py:166
  360.2 9.3 %convert_bitcast_fusion.1 = bf16[128,1,128,128]{3,2,0,1:T(8,128)(2,1)} fusion(bf16[128,256,128]{2,1,0:T(8,128)(2,1)} %gather_fusion.5, pred[128]{0:T(512)(128)(4,1)S(1)} %get-tuple-element.48, bf16[128,256,128]{2,1,0:T(8,128)(2,1)} %gather_fusion.2, pred[128]{0:T(512)(128)(4,1)S(1)} %get-tuple-element.49), kind=kOutput, calls=%fused_computation.32 | convolution fusion | flops 1084227584 | bytes 20971776 | tf_op jit(solution)/shard_map/rsk,rsn->skn/dot_general | solution.py:165
  369.5 6.3 %pad_maximum_fusion = bf16[128,2,128,128]{3,2,0,1:T(8,128)(2,1)} fusion(bf16[128,1,128,128]{3,2,0,1:T(8,128)(2,1)S(1)} %convert_bitcast_fusion, bf16[128,1,128,128]{3,2,0,1:T(8,128)(2,1)} %convert_bitcast_fusion.1), kind=kLoop, calls=%fused_computation.12 | loop fusion | flops 4194304 | bytes 16777216 | tf_op jit(solution)/shard_map/stack | solution.py:168
  379.5 7.1 %reduce-scatter.6.cloned.1.call-done = bf16[256,512]{0,1:T(8,128)(2,1)} async-done(((bf16[256,4096]{0,1:T(8,128)(2,1)}), bf16[256,512]{0,1:T(8,128)(2,1)}) %reduce-scatter.6.cloned.1.call-update) | async-done | bytes 262160 | tf_op jit(solution)/shard_map/reduce_scatter | solution.py:129
  388.4 214.7 %all-reduce.3.cloned.1.call-done = bf16[128,2,128,128]{3,2,0,1:T(8,128)(2,1)} async-done(((bf16[128,2,128,128]{3,2,0,1:T(8,128)(2,1)}), bf16[128,2,128,128]{3,2,0,1:T(8,128)(2,1)}) %all-reduce.3.cloned.1.call-update) | async-done | bytes 8388624
  (85 shorter events, 24.8 us)
Async XLA Ops:
  7.2 35.3 %all-gather.8.cloned.1.call-start = ((), (), s32[]{:S(2)}) async-start(), calls=%async_computation.6 | async-start | bytes 2359296 | tf_op jit(solution)/shard_map/all_gather | solution.py:138
  9.0 26.1 %copy-start = (bf16[128,1792]{1,0:T(8,128)(2,1)S(1)}, bf16[128,1792]{1,0:T(8,128)(2,1)}, u32[]{:S(2)}) copy-start(bf16[128,1792]{1,0:T(8,128)(2,1)} %param.14) | copy-start | bytes 1376260
  9.0 64.1 %all-gather.6.cloned.1.call-start = ((), (), s32[]{:S(2)}) async-start(), calls=%async_computation.4 | async-start | bytes 2359296 | tf_op jit(solution)/shard_map/all_gather | solution.py:110
  22.9 109.8 %all-to-all-start = ((bf16[32,4,128,128]{3,2,1,0:T(8,128)(2,1)}), bf16[32,4,128,128]{3,2,1,0:T(8,128)(2,1)}, u32[]{:S(2)}, u32[]{:S(2)}) async-start(bf16[32,4,128,128]{3,2,1,0:T(8,128)(2,1)} %stack.11), calls=%async_computation | async-start | bytes 8388608 | tf_op jit(solution)/shard_map/all_to_all | solution.py:13
  35.1 135.3 %all-gather.4.cloned.1.call-start = ((), (), s32[]{:S(2)}) async-start(), calls=%async_computation.3 | async-start | bytes 4325376 | tf_op jit(solution)/shard_map/all_gather | solution.py:82
  37.7 340.0 %reduce-scatter.8.cloned.1.call-start = ((), (), s32[]{:S(2)}) async-start(), calls=%async_computation.7 | async-start | bytes 2359296 | tf_op jit(solution)/shard_map/reduce_scatter | solution.py:151
  288.8 97.8 %reduce-scatter.6.cloned.1.call-start = ((), (), s32[]{:S(2)}) async-start(), calls=%async_computation.5 | async-start | bytes 2359296 | tf_op jit(solution)/shard_map/reduce_scatter | solution.py:129
  352.1 251.0 %all-reduce.3.cloned.1.call-start = ((), (), s32[]{:S(2)}) async-start(), calls=%async_computation.8 | async-start | bytes 16777216
  375.8 0.7 copy-start.5
  375.8 228.3 %copy-start.1 = (pred[4]{0:T(512)(128)(4,1)S(1)}, pred[4]{0:T(512)(128)(4,1)}, u32[]{:S(2)}) copy-start(pred[4]{0:T(512)(128)(4,1)} %get-tuple-element.28) | copy-start | bytes 16
  375.8 228.3 %copy-start.2 = (pred[4]{0:T(512)(128)(4,1)S(1)}, pred[4]{0:T(512)(128)(4,1)}, u32[]{:S(2)}) copy-start(pred[4]{0:T(512)(128)(4,1)} %get-tuple-element.32) | copy-start | bytes 16
  375.8 228.5 %copy-start.4 = (s32[4]{0:T(128)S(1)}, s32[4]{0:T(128)}, u32[]{:S(2)}) copy-start(s32[4]{0:T(128)} %get-tuple-element.30) | copy-start | bytes 52
  375.8 230.9 %copy-start.3 = (s32[4]{0:T(128)S(1)}, s32[4]{0:T(128)}, u32[]{:S(2)}) copy-start(s32[4]{0:T(128)} %get-tuple-element.46) | copy-start | bytes 52
Sparse Core Ops, SparseCore 0:
  10.4 31.9 all-gather.7
  44.9 28.2 all-gather.5
  76.3 87.5 all-gather.3
  288.9 34.2 reduce-scatter.7
  352.2 34.3 reduce-scatter.5
  390.1 212.8 all-reduce.2
